TPU v7x, 32 devices: a whole 2x2x4 slice. The times are simulated.
32 devices in a mesh: groups: 2 (over y), tensor: 16 (over z, x, core).
Axes of the slice: x: 2, y: 2, z: 4, core: 2. Of those that a mesh axis runs over, the one named last changes fastest.
Arguments:
- normed_input: bfloat16 [16, 2, 8192], P('groups', None, 'tensor'), parts along dimension 0, may hold values from -6 to 6
- query_weight: bfloat16 [8192, 8192], P('tensor'), may hold values from -0.0625 to 0.0625
- query_gain: float32 [128], replicated, may hold values from 0.5 to 50
- image_cache: bfloat16 [32, 1601, 2048], P(('groups', 'tensor')), parts along dimension 0, may hold values from -18 to 18
- tile_count: int32 [16], P('groups'), parts along dimension 0, may hold values from 1 to 4, as said below
- image_first_slot: int32 [16], P('groups'), parts along dimension 0, may hold values from 0 to 15, as said below
- cross_tile_mask: int32 [16, 2, 4], P('groups'), parts along dimension 0, may hold values 0 or 1
- output_weight: bfloat16 [8192, 8192], P(None, 'tensor'), may hold values from -0.0625 to 0.0625
- output_gate: float32 [1], replicated, may hold values from 0.3 to 1.5
Outputs:
- cross_output: bfloat16 [16, 2, 8192], P('groups', None, 'tensor'), parts along dimension 0
There are 2 independent parts, one for each index of `groups`. A program takes and returns all parts, laid end to end along the dimension named above; an argument that names none is the same for every part. Nothing has to cross between parts.
Inputs may be any that keep to these rules, and one draw needn't show every extreme that they name: tile_count sums to 16; some row has 4 tiles. Row r's tiles are pool slots image_first_slot[r] to image_first_slot[r] + tile_count[r] - 1; the images fill all 16 slots, each slot belonging to exactly one row.
All inputs are finite; a program needn't handle non-finite values.
Results may differ from a plain program's by a relative error of at most 0.0077.
Values may be sent and summed in bfloat16 or wider, within the bound.
A program may use at most 64 MiB of HBM per device.

v0:
```python
import math
import jax
import jax.numpy as jnp
from jax import lax
from jax.sharding import PartitionSpec as P

EPSILON = 1e-05
NEGATIVE_FLOOR = -1e30


def membership(image_first_slot, tile_count, pool_slots):
    ends = image_first_slot + tile_count
    return (pool_slots[:, None] >= image_first_slot[None, :]) & (
        pool_slots[:, None] < ends[None, :]
    )


def active_status(member_flag, image_first_slot, cross_tile_mask, pool_slots):
    member_int = member_flag.astype(jnp.int32)
    tile_index = jnp.sum(member_int * (pool_slots[:, None] - image_first_slot[None, :]), axis=1)
    row_masks = jnp.sum(member_int[:, :, None, None] * cross_tile_mask[None], axis=1)
    positions = jnp.arange(cross_tile_mask.shape[2], dtype=jnp.int32)
    chosen = jnp.sum(
        jnp.where(positions[None, None, :] == tile_index[:, None, None], row_masks, 0), axis=2
    )
    return (tile_index[:, None] == 0) | (chosen == 1)


def tile_partial(query_rows, cache_tile, head_size):
    steps = query_rows.shape[0]
    kv_width = cache_tile.shape[1] // 2
    kv_heads = kv_width // head_size
    group = query_rows.shape[1] // kv_width
    grouped = query_rows.reshape(steps, kv_heads, group, head_size)
    keys = cache_tile[:, :kv_width].reshape(-1, kv_heads, head_size)
    values = cache_tile[:, kv_width:].reshape(-1, kv_heads, head_size)
    scores = jnp.einsum("skgd,tkd->skgt", grouped, keys, preferred_element_type=jnp.float32) * (
        1.0 / math.sqrt(head_size)
    )
    tops = jnp.max(scores, axis=3)
    weights = jnp.exp(scores - tops[..., None]).astype(jnp.bfloat16)
    totals = jnp.sum(weights.astype(jnp.float32), axis=3)
    mixed = jnp.einsum("skgt,tkd->skgd", weights, values, preferred_element_type=jnp.float32)
    return (tops.reshape(steps, -1), totals.reshape(steps, -1), mixed.reshape(steps, -1))


def finish(numer_pairs, denom_pairs, head_size):
    pairs = numer_pairs.shape[0]
    heads = denom_pairs.shape[1]
    shaped = numer_pairs.reshape(pairs, heads, head_size) / denom_pairs[..., None]
    return shaped.astype(jnp.bfloat16).reshape(pairs, heads * head_size)


def body(
    normed_input,
    query_weight,
    query_gain,
    image_cache,
    tile_count,
    image_first_slot,
    cross_tile_mask,
    output_weight,
    output_gate,
):
    rows, steps, local_width = normed_input.shape
    head_size = query_gain.shape[0]
    heads = query_weight.shape[1] // head_size
    slot_count = image_cache.shape[0]
    flattened = normed_input.reshape(rows * steps, local_width)
    query = lax.psum_scatter(
        jnp.dot(flattened, query_weight, preferred_element_type=jnp.float32),
        "tensor",
        scatter_dimension=0,
        tiled=True,
    )
    shaped = query.reshape(slot_count, heads, head_size)
    normed = (
        shaped * lax.rsqrt(jnp.mean(shaped * shaped, axis=2, keepdims=True) + EPSILON) * query_gain
    )
    normed = normed.astype(jnp.bfloat16).reshape(slot_count, heads * head_size)
    all_queries = lax.all_gather(normed, "tensor", axis=0, tiled=True)
    target_device = lax.axis_index("tensor")
    pool_slots = target_device * slot_count + jnp.arange(slot_count, dtype=jnp.int32)
    member_flag = membership(image_first_slot, tile_count, pool_slots)
    active_entry = active_status(member_flag, image_first_slot, cross_tile_mask, pool_slots)
    by_row = all_queries.reshape(rows, steps * heads * head_size)
    selected = jnp.dot(member_flag.astype(jnp.bfloat16), by_row, preferred_element_type=jnp.float32)
    selected = selected.astype(jnp.bfloat16).reshape(slot_count, steps, heads * head_size)

    def slot_term(operands):
        return tile_partial(operands[0], operands[1], head_size)

    tops, totals, mixed = lax.map(slot_term, (selected, image_cache))
    masked = jnp.where(active_entry[:, :, None], tops, NEGATIVE_FLOOR)
    pair_index = target_device * slot_count + jnp.arange(slot_count, dtype=jnp.int32)
    pair_row = pair_index // steps
    pair_step = pair_index % steps
    gathered_tops, gathered_totals, gathered_mixed = (
        lax.all_gather(masked, "tensor", axis=0, tiled=True),
        lax.all_gather(totals, "tensor", axis=0, tiled=True),
        lax.all_gather(mixed, "tensor", axis=0, tiled=True),
    )
    all_slots = gathered_tops.shape[0]
    every_slot = jnp.arange(all_slots, dtype=jnp.int32)
    full_member = membership(image_first_slot, tile_count, every_slot)
    slot_pick = full_member[:, pair_row]
    step_pick = jnp.arange(steps, dtype=jnp.int32)[None, :] == pair_step[:, None]
    chosen = slot_pick[:, :, None] & step_pick[None, :, :]
    spread = jnp.where(chosen[..., None], gathered_tops[:, None, :, :], NEGATIVE_FLOOR)
    pair_max = jnp.max(spread, axis=(0, 2))
    weights = jnp.where(chosen[..., None], jnp.exp(spread - pair_max[None, :, None, :]), 0.0)
    denom_pairs = jnp.sum(weights * gathered_totals[:, None, :, :], axis=(0, 2))
    mixed_heads = gathered_mixed.reshape(all_slots, steps, heads, head_size)
    numer_pairs = jnp.einsum(
        "spth,sthd->phd", weights, mixed_heads, precision=lax.Precision.HIGHEST
    )
    numer_pairs = numer_pairs.reshape(slot_count, heads * head_size)
    attended = finish(numer_pairs, denom_pairs, head_size)
    projected = jnp.dot(
        lax.all_gather(attended, "tensor", axis=0, tiled=True),
        output_weight,
        preferred_element_type=jnp.float32,
    )
    result = jnp.tanh(output_gate[0]) * projected
    return result.astype(jnp.bfloat16).reshape(rows, steps, -1)


def solution(mesh):
    return jax.shard_map(
        body,
        mesh=mesh,
        in_specs=(
            P("groups", None, "tensor"),
            P("tensor", None),
            P(),
            P(("groups", "tensor"), None, None),
            P("groups"),
            P("groups"),
            P("groups", None, None),
            P(None, "tensor"),
            P(),
        ),
        out_specs=P("groups", None, "tensor"),
        check_vma=False,
    )
```

profile of v0, /device:TPU:0, one launch (start us, length us, event | category | flops | bytes accessed | tf_op | source)
XLA Modules:
  0.0 217.2 jit_solution(3710583259249691234)
XLA Ops:
  6.5 0.0 all-reduce.3.cloned.1.call-start
  6.5 0.7 reshape.264
  7.3 5.4 %fusion.27 = f32[16,8192]{1,0:T(8,128)} fusion(bf16[16,512]{1,0:T(8,128)(2,1)S(1)} %reshape.264, bf16[512,8192]{1,0:T(8,128)(2,1)} %param.10), kind=kOutput, calls=%fused_computation.45 | convolution fusion | flops 134217728 | bytes 8929280 | tf_op jit(solution)/shard_map/dot_general | solution.py:71
  12.6 0.0 all-reduce.3.cloned.1.call-update
  12.7 0.0 all-gather.4.cloned.1.call-start
  12.7 3.7 %fusion.25 = (bf16[1601,1024]{1,0:T(8,128)(2,1)S(1)}, bf16[1601,1024]{1,0:T(8,128)(2,1)S(1)}) fusion(bf16[1601,2048]{1,0:T(8,128)(2,1)} %bitcast.51), kind=kLoop, calls=%fused_computation.43 | loop fusion | bytes 13115392 | tf_op jit(solution)/shard_map/while/body/eval_jaxpr/slice | solution.py:36
  16.4 0.9 copy.38
  17.3 0.3 slice_bitcast_fusion.1
  17.6 0.9 copy.39
  18.4 0.0 copy-start.6
  18.4 0.0 copy-start.2
  18.4 0.0 copy-start.5
  18.5 0.0 copy-start.4
  18.5 1.8 slice_bitcast_fusion
  20.3 0.0 copy-done.6
  20.3 0.6 dynamic-slice.4
  20.9 0.0 copy-done.2
  20.9 0.0 copy-done.5
  20.9 0.6 select_reduce_fusion.1
  21.5 84.8 %all-reduce.3.cloned.1.call-done = f32[16,8192]{1,0:T(8,128)} async-done(((f32[16,8192]{1,0:T(8,128)}), f32[16,8192]{1,0:T(8,128)}) %all-reduce.3.cloned.1.call-update) | async-done | bytes 524304
  106.3 1.6 dynamic-slice_multiply_fusion
  107.9 0.1 reduce_sum.55
  108.0 0.0 copy-done.4
  108.0 0.1 mul.75
  108.1 1.7 convert_bitcast_fusion
  109.8 23.6 %all-gather = bf16[16,1,8192]{2,1,0:T(2,128)(2,1)} all-gather(bf16[1,1,8192]{2,1,0:T(2,128)(2,1)S(1)} %convert_bitcast_fusion), channel_id=1, replica_groups=mesh['groups'=2,'tensor'=16] {'tensor'}, dimensions={0}, use_global_device_ids=true | all-gather | bytes 278528 | tf_op jit(solution)/shard_map/all_gather | solution.py:81
  133.4 3.2 %reduce.12 = bf16[16,8192]{1,0:T(8,128)(2,1)} reduce(bf16[16,1,8192]{2,1,0:T(2,128)(2,1)} %all-gather, bf16[]{:T(256)} %constant.103), dimensions={1}, to_apply=%all-gather.reduce_sub_computation | reduce | bytes 524290 | tf_op jit(solution)/shard_map/all_gather | solution.py:81
  136.6 1.1 reshape.265
  137.7 0.0 copy-start
  137.7 0.2 fusion.21
  137.9 1.1 fusion.26
  139.0 0.0 copy-start.1
  139.0 0.0 copy-start.3
  139.0 0.6 copy-done
  139.6 1.2 fusion.10
  140.8 0.0 copy-done.1
  140.8 0.7 broadcast_in_dim.87
  141.5 0.0 all-gather.4.cloned.1.call-update
  141.5 0.6 iota_compare_fusion.2
  143.4 0.1 fusion.20
  143.4 0.0 copy-done.3
  143.5 0.2 multiply_reduce_fusion.1
  143.6 0.1 select_reduce_fusion
  143.7 0.1 broadcast_and_fusion
  143.8 1.4 convert_reduce_fusion
  145.3 0.1 broadcast_in_dim.97
  145.3 0.1 broadcast_in_dim.93
  145.4 17.5 %all_gather.18 = f32[16,2,64]{2,1,0:T(2,128)S(1)} all-gather(f32[1,2,64]{2,1,0:T(2,128)S(1)} %broadcast_in_dim.97), channel_id=1, replica_groups=mesh['groups'=2,'tensor'=16] {'tensor'}, dimensions={0}, use_global_device_ids=true | all-gather | bytes 8704 | tf_op jit(solution)/shard_map/all_gather | solution.py:100
  162.9 0.1 broadcast_select_fusion.1
  163.0 19.0 %all_gather.17 = f32[16,2,64]{2,1,0:T(2,128)S(1)} all-gather(f32[1,2,64]{2,1,0:T(2,128)S(1)} %broadcast_select_fusion.1), channel_id=1, replica_groups=mesh['groups'=2,'tensor'=16] {'tensor'}, dimensions={0}, use_global_device_ids=true | all-gather | bytes 8704 | tf_op jit(solution)/shard_map/all_gather | solution.py:99
  181.9 0.1 fusion.19
  182.0 0.1 multiply_reduce_fusion
  182.1 0.1 copy.31
  182.2 0.0 all-gather.4.cloned.1.call-done
  182.3 2.1 reshape.269
  184.4 1.7 fusion.14
  186.1 0.1 divide_convert_fusion
  186.2 18.9 %all-gather.1 = bf16[16,1,8192]{2,1,0:T(2,128)(2,1)S(1)} all-gather(bf16[1,1,8192]{2,1,0:T(2,128)(2,1)S(1)} %reshape.298), channel_id=1, replica_groups=mesh['groups'=2,'tensor'=16] {'tensor'}, dimensions={0}, use_global_device_ids=true | all-gather | bytes 278528 | tf_op jit(solution)/shard_map/all_gather | solution.py:120
  205.1 4.6 %fusion.13 = bf16[16,512]{1,0:T(8,128)(2,1)S(1)} fusion(bf16[8192,512]{1,0:T(8,128)(2,1)} %param.16, bf16[16,1,8192]{2,1,0:T(2,128)(2,1)S(1)} %all-gather.1, f32[]{:T(128)} %bitcast), kind=kOutput, calls=%fused_computation.10 | convolution fusion | flops 134234112 | bytes 8667140 | tf_op jit(solution)/shard_map/dot_general | solution.py:119
  209.7 0.6 reshape.271
  (11 shorter events, 0.1 us)
Async XLA Ops:
  6.5 99.7 %all-reduce.3.cloned.1.call-start = ((), (), s32[]{:S(2)}) async-start(), calls=%async_computation.1 | async-start | bytes 1048576
  12.7 169.6 %all-gather.4.cloned.1.call-start = ((), (), s32[]{:S(2)}) async-start(), calls=%async_computation | async-start | bytes 1114112 | tf_op jit(solution)/shard_map/all_gather | solution.py:101
  18.4 1.9 copy-start.6
  18.4 2.4 %copy-start.2 = (s32[8]{0:T(128)S(1)}, s32[8]{0:T(128)}, u32[]{:S(2)}) copy-start(s32[8]{0:T(128)} %param.14) | copy-start | bytes 100
  18.4 2.4 %copy-start.5 = (s32[8]{0:T(128)S(1)}, s32[8]{0:T(128)}, u32[]{:S(2)}) copy-start(s32[8]{0:T(128)} %param.13) | copy-start | bytes 100
  18.5 89.6 %copy-start.4 = (f32[128]{0:T(128)S(1)}, f32[128]{0:T(128)}, u32[]{:S(2)}) copy-start(f32[128]{0:T(128)} %param.11) | copy-start | bytes 1540
  137.7 1.9 copy-start
  139.0 1.8 copy-start.1
  139.0 4.4 %copy-start.3 = (s32[8,2,4]{0,2,1:T(4,128)S(1)}, s32[8,2,4]{0,2,1:T(4,128)}, u32[]{:S(2)}) copy-start(s32[8,2,4]{0,2,1:T(4,128)} %param.15) | copy-start | bytes 772
Sparse Core Ops, SparseCore 0:
  12.8 93.4 all-reduce.2
  141.6 35.1 all-gather.3
where the time goes:
time: 218 us; the launch traced here: 217 us
  waiting for transfers between devices  84.8 us (39%)
  blocking collectives  78.9 us (36%)
  between operations  14.9 us (7%)
  local copies, waits for them, and re-layouts  14.2 us (7%)
  matrix products  14.2 us (7%)
  other arithmetic  10.1 us (5%)
    unnamed x3, waiting for transfers between devices  84.8 us
    all_gather x1, blocking collectives, body(): all_queries = lax.all_gather(normed, 'tensor', axis=0, tiled=True)  23.6 us
    all_gather x1, blocking collectives, body(): lax.all_gather(masked, 'tensor', axis=0, tiled=True)  19 us
    all_gather x1, blocking collectives, body(): lax.all_gather(attended, 'tensor', axis=0, tiled=True)  18.9 us
    all_gather x1, blocking collectives, body(): lax.all_gather(totals, 'tensor', axis=0, tiled=True)  17.5 us
    dot_general x1, matrix products, body(): jnp.dot(flattened, query_weight, preferred_element_type=jnp.float32)  5.38 us
    dot_general x1, matrix products, body(): jnp.dot(lax.all_gather(attended, 'tensor', axis=0, tiled=True), output_we...  4.62 us
  transfers between devices with their start and end apart: 2, of which 1 were waited for; matrix products, arithmetic and copies ran while one was open for 5% of the time, Pallas kernels for 0%

commit v1 on v0

--- a/solution.py
+++ b/solution.py
@@ -6,6 +6,19 @@
 
 EPSILON = 1e-05
 NEGATIVE_FLOOR = -1e30
+
+
+def collect(array, axis, dim):
+    ways = lax.axis_size(axis)
+    up = [(d, (d + 1) % ways) for d in range(ways)]
+    down = [(d, (d - 1) % ways) for d in range(ways)]
+    earlier, later = ([array], [array])
+    for _ in range(ways // 2):
+        earlier.append(lax.ppermute(earlier[-1], axis, up))
+    for _ in range((ways - 1) // 2):
+        later.append(lax.ppermute(later[-1], axis, down))
+    line = jnp.concatenate([*earlier[::-1], *later[1:]], axis=dim)
+    return jnp.roll(line, (lax.axis_index(axis) - ways // 2) * array.shape[dim], axis=dim)
 
 
 def membership(image_first_slot, tile_count, pool_slots):
@@ -96,7 +109,7 @@
     pair_row = pair_index // steps
     pair_step = pair_index % steps
     gathered_tops, gathered_totals, gathered_mixed = (
-        lax.all_gather(masked, "tensor", axis=0, tiled=True),
+        collect(masked, "tensor", 0),
         lax.all_gather(totals, "tensor", axis=0, tiled=True),
         lax.all_gather(mixed, "tensor", axis=0, tiled=True),
     )

time: 218 us -> 275 us (1.26)
  waiting for transfers between devices: 84.8 us -> 125 us
  starting transfers between devices: 0.04 us -> 28.4 us
  blocking collectives: 78.9 us -> 62.4 us
  matrix products: 14.2 us -> 18.1 us
    all_gather x1, waiting for transfers between devices: 0.02 us -> 32.6 us  [body(): lax.all_gather(mixed, 'tensor', axis=0, tiled=True)]
    ppermute x0 -> x15, starting transfers between devices: none -> 28.4 us  [the longest x7 28 us: collect(): later.append(lax.ppermute(later[-1], axis, down))]
    all_gather x1 -> x0, blocking collectives: 19 us -> none  [body(): lax.all_gather(masked, 'tensor', axis=0, tiled=True)]
    ppermute x0 -> x15, waiting for transfers between devices: none -> 10.4 us  [the longest x8 7.54 us: collect(): earlier.append(lax.ppermute(earlier[-1], axis, up))]
    unnamed x3, waiting for transfers between devices: 84.8 us -> 81.6 us
  transfers between devices with their start and end apart: 2 -> 17, of which waited for: 1 -> 10; matrix products, arithmetic and copies ran while one was open for 5% -> 6% of each run, Pallas kernels for 0% -> 0%
where the time goes in v1:
time: 275 us; the launch traced here: 274 us
  waiting for transfers between devices  125 us (45%)
  blocking collectives  62.4 us (23%)
  starting transfers between devices  28.4 us (10%)
  matrix products  18.1 us (7%)
  local copies, waits for them, and re-layouts  15 us (5%)
  between operations  15 us (5%)
  other arithmetic  11 us (4%)
    unnamed x3, waiting for transfers between devices  81.6 us
    all_gather x1, waiting for transfers between devices, body(): lax.all_gather(mixed, 'tensor', axis=0, tiled=True)  32.6 us
    ppermute x7, starting transfers between devices, collect(): later.append(lax.ppermute(later[-1], axis, down))  28 us
    all_gather x1, blocking collectives, body(): all_queries = lax.all_gather(normed, 'tensor', axis=0, tiled=True)  23.6 us
    all_gather x1, blocking collectives, body(): lax.all_gather(attended, 'tensor', axis=0, tiled=True)  20.8 us
    all_gather x1, blocking collectives, body(): lax.all_gather(totals, 'tensor', axis=0, tiled=True)  18 us
    ppermute x8, waiting for transfers between devices, collect(): earlier.append(lax.ppermute(earlier[-1], axis, up))  7.54 us
  transfers between devices with their start and end apart: 17, of which 10 were waited for; matrix products, arithmetic and copies ran while one was open for 6% of the time, Pallas kernels for 0%

profile of v1, /device:TPU:0, one launch (start us, length us, event | category | flops | bytes accessed | tf_op | source)
XLA Modules:
  0.0 274.5 jit_solution(336167784993820770)
XLA Ops:
  6.5 0.7 reshape.264
  7.3 5.4 %fusion.27 = f32[16,8192]{1,0:T(8,128)} fusion(bf16[16,512]{1,0:T(8,128)(2,1)S(1)} %reshape.264, bf16[512,8192]{1,0:T(8,128)(2,1)} %param.10), kind=kOutput, calls=%fused_computation.77 | convolution fusion | flops 134217728 | bytes 8929280 | tf_op jit(solution)/shard_map/dot_general | solution.py:84
  12.7 0.0 all-gather.4.cloned.1.call-start
  12.7 3.7 %fusion.25 = (bf16[1601,1024]{1,0:T(8,128)(2,1)S(1)}, bf16[1601,1024]{1,0:T(8,128)(2,1)S(1)}) fusion(bf16[1601,2048]{1,0:T(8,128)(2,1)} %bitcast.51), kind=kLoop, calls=%fused_computation.75 | loop fusion | bytes 13115392 | tf_op jit(solution)/shard_map/while/body/eval_jaxpr/slice | solution.py:49
  16.4 0.9 copy.38
  17.3 1.8 slice_bitcast_fusion.1
  19.1 0.6 select_reduce_fusion.1
  19.8 0.6 iota_compare_fusion.2
  21.1 0.9 copy.39
  22.0 0.3 slice_bitcast_fusion
  22.2 0.4 copy-done.2
  22.6 0.1 multiply_reduce_fusion.1
  22.8 0.1 select_reduce_fusion
  22.9 0.5 iota_compare_fusion.3
  23.4 0.7 dynamic-slice.4
  24.1 0.6 fusion.20
  24.7 81.5 %all-reduce.3.cloned.1.call-done = f32[16,8192]{1,0:T(8,128)} async-done(((f32[16,8192]{1,0:T(8,128)}), f32[16,8192]{1,0:T(8,128)}) %all-reduce.3.cloned.1.call-update) | async-done | bytes 524304
  106.3 1.7 dynamic-slice_multiply_fusion
  107.9 0.1 reduce_sum.55
  108.1 0.1 mul.75
  108.2 1.7 convert_bitcast_fusion
  109.9 23.6 %all-gather = bf16[16,1,8192]{2,1,0:T(2,128)(2,1)} all-gather(bf16[1,1,8192]{2,1,0:T(2,128)(2,1)S(1)} %convert_bitcast_fusion), channel_id=1, replica_groups=mesh['groups'=2,'tensor'=16] {'tensor'}, dimensions={0}, use_global_device_ids=true | all-gather | bytes 278528 | tf_op jit(solution)/shard_map/all_gather | solution.py:94
  133.5 3.3 %reduce.12 = bf16[16,8192]{1,0:T(8,128)(2,1)} reduce(bf16[16,1,8192]{2,1,0:T(2,128)(2,1)} %all-gather, bf16[]{:T(256)} %constant.127), dimensions={1}, to_apply=%all-gather.reduce_sub_computation | reduce | bytes 524290 | tf_op jit(solution)/shard_map/all_gather | solution.py:94
  136.7 1.1 reshape.265
  137.8 0.2 fusion.21
  138.0 3.9 %fusion.26 = (f32[2,8,8]{2,0,1:T(2,128)S(1)}, f32[2,8,8,1601]{3,2,0,1:T(8,128)}) fusion(bf16[1601,8,128,1]{2,1,0,3:T(8,128)(2,1)} %slice_bitcast_fusion.1, bf16[2,8,8,128]{3,2,1,0:T(8,128)(2,1)S(1)} %bitcast.53), kind=kOutput, calls=%fused_computation.76 | convolution fusion | flops 52871296 | bytes 4131840 | tf_op jit(solution)/shard_map/while/body/eval_jaxpr/skgd,tkd->skgt/dot_general | solution.py:50
  141.9 0.1 broadcast_in_dim.93
  142.0 0.1 broadcast_select_fusion
  142.0 0.4 collective-permute-start
  142.4 5.3 %collective-permute-done = f32[1,2,64]{2,1,0:T(2,128)S(1)} collective-permute-done((f32[1,2,64]{2,1,0:T(2,128)S(1)}, f32[1,2,64]{2,1,0:T(2,128)S(1)}, u32[]{:S(2)}, u32[]{:S(2)}) %collective-permute-start) | collective-permute-done | bytes 544 | tf_op jit(solution)/shard_map/ppermute | solution.py:17
  147.7 0.7 dynamic-slice_bitcast_fusion
  148.4 4.4 %collective-permute-start.8 = (f32[1,2,64]{2,1,0:T(2,128)S(1)}, f32[1,2,64]{2,1,0:T(2,128)S(1)}, u32[]{:S(2)}, u32[]{:S(2)}) collective-permute-start(f32[1,2,64]{2,1,0:T(2,128)S(1)} %broadcast_select_fusion), channel_id=1, source_target_pairs={{0,15},{1,0},{2,1},{3,2},{4,3},{5,4},{6,5},{7,6},{8,7},{9,8},{10,9... | collective-permute-start | bytes 1544 | tf_op jit(solution)/shard_map/ppermute | solution.py:19
  152.9 0.6 collective-permute-done.1
  153.4 0.7 broadcast_and_fusion
  154.1 0.0 collective-permute-done.8
  154.2 4.4 %collective-permute-start.9 = (f32[1,2,64]{2,1,0:T(2,128)S(1)}, f32[1,2,64]{2,1,0:T(2,128)S(1)}, u32[]{:S(2)}, u32[]{:S(2)}) collective-permute-start(f32[1,2,64]{2,1,0:T(2,128)S(1)} %collective-permute-done.8), channel_id=1, source_target_pairs={{0,15},{1,0},{2,1},{3,2},{4,3},{5,4},{6,5},{7,6},{8,7},{9,8},{10,9... | collective-permute-start | bytes 1544 | tf_op jit(solution)/shard_map/ppermute | solution.py:19
  158.6 0.6 collective-permute-done.2
  159.1 0.7 collective-permute-done.9
  159.9 4.4 %collective-permute-start.10 = (f32[1,2,64]{2,1,0:T(2,128)S(1)}, f32[1,2,64]{2,1,0:T(2,128)S(1)}, u32[]{:S(2)}, u32[]{:S(2)}) collective-permute-start(f32[1,2,64]{2,1,0:T(2,128)S(1)} %collective-permute-done.9), channel_id=1, source_target_pairs={{0,15},{1,0},{2,1},{3,2},{4,3},{5,4},{6,5},{7,6},{8,7},{9,8},{10,9... | collective-permute-start | bytes 1544 | tf_op jit(solution)/shard_map/ppermute | solution.py:19
  164.3 0.6 collective-permute-done.3
  165.6 4.5 %collective-permute-start.11 = (f32[1,2,64]{2,1,0:T(2,128)S(1)}, f32[1,2,64]{2,1,0:T(2,128)S(1)}, u32[]{:S(2)}, u32[]{:S(2)}) collective-permute-start(f32[1,2,64]{2,1,0:T(2,128)S(1)} %collective-permute-done.10), channel_id=1, source_target_pairs={{0,15},{1,0},{2,1},{3,2},{4,3},{5,4},{6,5},{7,6},{8,7},{9,8},{10,9... | collective-permute-start | bytes 1544 | tf_op jit(solution)/shard_map/ppermute | solution.py:19
  170.0 0.5 collective-permute-done.4
  170.5 2.3 fusion.10
  172.9 4.5 %collective-permute-start.12 = (f32[1,2,64]{2,1,0:T(2,128)S(1)}, f32[1,2,64]{2,1,0:T(2,128)S(1)}, u32[]{:S(2)}, u32[]{:S(2)}) collective-permute-start(f32[1,2,64]{2,1,0:T(2,128)S(1)} %collective-permute-done.11), channel_id=1, source_target_pairs={{0,15},{1,0},{2,1},{3,2},{4,3},{5,4},{6,5},{7,6},{8,7},{9,8},{10,9... | collective-permute-start | bytes 1544 | tf_op jit(solution)/shard_map/ppermute | solution.py:19
  177.4 0.3 convert_reduce_fusion
  177.6 0.1 broadcast_in_dim.97
  177.7 0.9 collective-permute-done.12
  178.6 4.4 %collective-permute-start.13 = (f32[1,2,64]{2,1,0:T(2,128)S(1)}, f32[1,2,64]{2,1,0:T(2,128)S(1)}, u32[]{:S(2)}, u32[]{:S(2)}) collective-permute-start(f32[1,2,64]{2,1,0:T(2,128)S(1)} %collective-permute-done.12), channel_id=1, source_target_pairs={{0,15},{1,0},{2,1},{3,2},{4,3},{5,4},{6,5},{7,6},{8,7},{9,8},{10,9... | collective-permute-start | bytes 1544 | tf_op jit(solution)/shard_map/ppermute | solution.py:19
  183.0 18.0 %all_gather.14 = f32[16,2,64]{2,1,0:T(2,128)S(1)} all-gather(f32[1,2,64]{2,1,0:T(2,128)S(1)} %broadcast_in_dim.97), channel_id=1, replica_groups=mesh['groups'=2,'tensor'=16] {'tensor'}, dimensions={0}, use_global_device_ids=true | all-gather | bytes 8704 | tf_op jit(solution)/shard_map/all_gather | solution.py:113
  201.1 0.7 broadcast_in_dim.87
  201.8 1.4 collective-permute-start.14
  203.3 0.1 constant_dynamic-update-slice_fusion.23
  203.4 1.1 collective-permute-done.14
  204.6 0.1 constant_dynamic-update-slice_fusion.7
  204.7 0.1 fusion.19
  204.8 0.1 multiply_reduce_fusion
  204.9 0.1 copy.31
  205.0 32.6 %all-gather.4.cloned.1.call-done = f32[16,2,8192]{2,1,0:T(2,128)} async-done(((f32[1,2,8192]{2,1,0:T(2,128)}), f32[16,2,8192]{2,1,0:T(2,128)}) %all-gather.4.cloned.1.call-update) | async-done | bytes 1048592 | tf_op jit(solution)/shard_map/all_gather | solution.py:114
  237.7 2.1 reshape.269
  239.8 1.7 fusion.14
  241.5 0.1 divide_convert_fusion
  241.6 20.8 %all-gather.1 = bf16[16,1,8192]{2,1,0:T(2,128)(2,1)S(1)} all-gather(bf16[1,1,8192]{2,1,0:T(2,128)(2,1)S(1)} %reshape.298), channel_id=1, replica_groups=mesh['groups'=2,'tensor'=16] {'tensor'}, dimensions={0}, use_global_device_ids=true | all-gather | bytes 278528 | tf_op jit(solution)/shard_map/all_gather | solution.py:133
  262.4 4.6 %fusion.13 = bf16[16,512]{1,0:T(8,128)(2,1)S(1)} fusion(bf16[8192,512]{1,0:T(8,128)(2,1)} %param.16, bf16[16,1,8192]{2,1,0:T(2,128)(2,1)S(1)} %all-gather.1, f32[]{:T(128)} %bitcast), kind=kOutput, calls=%fused_computation.10 | convolution fusion | flops 134234112 | bytes 8667140 | tf_op jit(solution)/shard_map/dot_general | solution.py:132
  267.0 0.6 reshape.271
  (66 shorter events, 0.4 us)
Async XLA Ops:
  6.5 99.7 %all-reduce.3.cloned.1.call-start = ((), (), s32[]{:S(2)}) async-start(), calls=%async_computation.1 | async-start | bytes 1048576
  12.7 225.0 %all-gather.4.cloned.1.call-start = ((), (), s32[]{:S(2)}) async-start(), calls=%async_computation | async-start | bytes 1114112 | tf_op jit(solution)/shard_map/all_gather | solution.py:114
  17.3 1.8 copy-start.1
  17.3 1.8 copy-start.4
  21.9 0.7 copy-start.2
  21.9 1.5 copy-start.5
  22.0 86.1 %copy-start.3 = (f32[128]{0:T(128)S(1)}, f32[128]{0:T(128)}, u32[]{:S(2)}) copy-start(f32[128]{0:T(128)} %param.11) | copy-start | bytes 1540
  142.0 5.7 %collective-permute-start = (f32[1,2,64]{2,1,0:T(2,128)S(1)}, f32[1,2,64]{2,1,0:T(2,128)S(1)}, u32[]{:S(2)}, u32[]{:S(2)}) collective-permute-start(f32[1,2,64]{2,1,0:T(2,128)S(1)} %broadcast_select_fusion), channel_id=1, source_target_pairs={{0,1},{1,2},{2,3},{3,4},{4,5},{5,6},{6,7},{7,8},{8,9},{9,10},{10,1... | collective-permute-start | bytes 1544 | tf_op jit(solution)/shard_map/ppermute | solution.py:17
  147.7 5.7 %collective-permute-start.1 = (f32[1,2,64]{2,1,0:T(2,128)S(1)}, f32[1,2,64]{2,1,0:T(2,128)S(1)}, u32[]{:S(2)}, u32[]{:S(2)}) collective-permute-start(f32[1,2,64]{2,1,0:T(2,128)S(1)} %collective-permute-done), channel_id=1, source_target_pairs={{0,1},{1,2},{2,3},{3,4},{4,5},{5,6},{6,7},{7,8},{8,9},{9,10},{10,1... | collective-permute-start | bytes 1544 | tf_op jit(solution)/shard_map/ppermute | solution.py:17
  148.4 5.7 %collective-permute-start.8 = (f32[1,2,64]{2,1,0:T(2,128)S(1)}, f32[1,2,64]{2,1,0:T(2,128)S(1)}, u32[]{:S(2)}, u32[]{:S(2)}) collective-permute-start(f32[1,2,64]{2,1,0:T(2,128)S(1)} %broadcast_select_fusion), channel_id=1, source_target_pairs={{0,15},{1,0},{2,1},{3,2},{4,3},{5,4},{6,5},{7,6},{8,7},{9,8},{10,9... | collective-permute-start | bytes 1544 | tf_op jit(solution)/shard_map/ppermute | solution.py:19
  153.4 5.7 %collective-permute-start.2 = (f32[1,2,64]{2,1,0:T(2,128)S(1)}, f32[1,2,64]{2,1,0:T(2,128)S(1)}, u32[]{:S(2)}, u32[]{:S(2)}) collective-permute-start(f32[1,2,64]{2,1,0:T(2,128)S(1)} %collective-permute-done.1), channel_id=1, source_target_pairs={{0,1},{1,2},{2,3},{3,4},{4,5},{5,6},{6,7},{7,8},{8,9},{9,10},{10,1... | collective-permute-start | bytes 1544 | tf_op jit(solution)/shard_map/ppermute | solution.py:17
  154.2 5.7 %collective-permute-start.9 = (f32[1,2,64]{2,1,0:T(2,128)S(1)}, f32[1,2,64]{2,1,0:T(2,128)S(1)}, u32[]{:S(2)}, u32[]{:S(2)}) collective-permute-start(f32[1,2,64]{2,1,0:T(2,128)S(1)} %collective-permute-done.8), channel_id=1, source_target_pairs={{0,15},{1,0},{2,1},{3,2},{4,3},{5,4},{6,5},{7,6},{8,7},{9,8},{10,9... | collective-permute-start | bytes 1544 | tf_op jit(solution)/shard_map/ppermute | solution.py:19
  159.1 5.7 %collective-permute-start.3 = (f32[1,2,64]{2,1,0:T(2,128)S(1)}, f32[1,2,64]{2,1,0:T(2,128)S(1)}, u32[]{:S(2)}, u32[]{:S(2)}) collective-permute-start(f32[1,2,64]{2,1,0:T(2,128)S(1)} %collective-permute-done.2), channel_id=1, source_target_pairs={{0,1},{1,2},{2,3},{3,4},{4,5},{5,6},{6,7},{7,8},{8,9},{9,10},{10,1... | collective-permute-start | bytes 1544 | tf_op jit(solution)/shard_map/ppermute | solution.py:17
  159.9 5.7 %collective-permute-start.10 = (f32[1,2,64]{2,1,0:T(2,128)S(1)}, f32[1,2,64]{2,1,0:T(2,128)S(1)}, u32[]{:S(2)}, u32[]{:S(2)}) collective-permute-start(f32[1,2,64]{2,1,0:T(2,128)S(1)} %collective-permute-done.9), channel_id=1, source_target_pairs={{0,15},{1,0},{2,1},{3,2},{4,3},{5,4},{6,5},{7,6},{8,7},{9,8},{10,9... | collective-permute-start | bytes 1544 | tf_op jit(solution)/shard_map/ppermute | solution.py:19
  164.8 5.7 %collective-permute-start.4 = (f32[1,2,64]{2,1,0:T(2,128)S(1)}, f32[1,2,64]{2,1,0:T(2,128)S(1)}, u32[]{:S(2)}, u32[]{:S(2)}) collective-permute-start(f32[1,2,64]{2,1,0:T(2,128)S(1)} %collective-permute-done.3), channel_id=1, source_target_pairs={{0,1},{1,2},{2,3},{3,4},{4,5},{5,6},{6,7},{7,8},{8,9},{9,10},{10,1... | collective-permute-start | bytes 1544 | tf_op jit(solution)/shard_map/ppermute | solution.py:17
  165.5 11.8 %copy-start = (f32[2,8,8,1601]{3,2,0,1:T(8,128)S(1)}, f32[2,8,8,1601]{3,2,0,1:T(8,128)}, u32[]{:S(2)}) copy-start(f32[2,8,8,1601]{3,2,0,1:T(8,128)} %get-tuple-element.41) | copy-start | bytes 2459140
  165.6 7.3 %collective-permute-start.11 = (f32[1,2,64]{2,1,0:T(2,128)S(1)}, f32[1,2,64]{2,1,0:T(2,128)S(1)}, u32[]{:S(2)}, u32[]{:S(2)}) collective-permute-start(f32[1,2,64]{2,1,0:T(2,128)S(1)} %collective-permute-done.10), channel_id=1, source_target_pairs={{0,15},{1,0},{2,1},{3,2},{4,3},{5,4},{6,5},{7,6},{8,7},{9,8},{10,9... | collective-permute-start | bytes 1544 | tf_op jit(solution)/shard_map/ppermute | solution.py:19
  170.5 6.8 %collective-permute-start.5 = (f32[1,2,64]{2,1,0:T(2,128)S(1)}, f32[1,2,64]{2,1,0:T(2,128)S(1)}, u32[]{:S(2)}, u32[]{:S(2)}) collective-permute-start(f32[1,2,64]{2,1,0:T(2,128)S(1)} %collective-permute-done.4), channel_id=1, source_target_pairs={{0,1},{1,2},{2,3},{3,4},{4,5},{5,6},{6,7},{7,8},{8,9},{9,10},{10,1... | collective-permute-start | bytes 1544 | tf_op jit(solution)/shard_map/ppermute | solution.py:17
  172.9 5.8 %collective-permute-start.12 = (f32[1,2,64]{2,1,0:T(2,128)S(1)}, f32[1,2,64]{2,1,0:T(2,128)S(1)}, u32[]{:S(2)}, u32[]{:S(2)}) collective-permute-start(f32[1,2,64]{2,1,0:T(2,128)S(1)} %collective-permute-done.11), channel_id=1, source_target_pairs={{0,15},{1,0},{2,1},{3,2},{4,3},{5,4},{6,5},{7,6},{8,7},{9,8},{10,9... | collective-permute-start | bytes 1544 | tf_op jit(solution)/shard_map/ppermute | solution.py:19
  177.3 5.7 %collective-permute-start.6 = (f32[1,2,64]{2,1,0:T(2,128)S(1)}, f32[1,2,64]{2,1,0:T(2,128)S(1)}, u32[]{:S(2)}, u32[]{:S(2)}) collective-permute-start(f32[1,2,64]{2,1,0:T(2,128)S(1)} %collective-permute-done.5), channel_id=1, source_target_pairs={{0,1},{1,2},{2,3},{3,4},{4,5},{5,6},{6,7},{7,8},{8,9},{9,10},{10,1... | collective-permute-start | bytes 1544 | tf_op jit(solution)/shard_map/ppermute | solution.py:17
  178.6 23.1 %collective-permute-start.13 = (f32[1,2,64]{2,1,0:T(2,128)S(1)}, f32[1,2,64]{2,1,0:T(2,128)S(1)}, u32[]{:S(2)}, u32[]{:S(2)}) collective-permute-start(f32[1,2,64]{2,1,0:T(2,128)S(1)} %collective-permute-done.12), channel_id=1, source_target_pairs={{0,15},{1,0},{2,1},{3,2},{4,3},{5,4},{6,5},{7,6},{8,7},{9,8},{10,9... | collective-permute-start | bytes 1544 | tf_op jit(solution)/shard_map/ppermute | solution.py:19
  183.0 20.1 %collective-permute-start.7 = (f32[1,2,64]{2,1,0:T(2,128)S(1)}, f32[1,2,64]{2,1,0:T(2,128)S(1)}, u32[]{:S(2)}, u32[]{:S(2)}) collective-permute-start(f32[1,2,64]{2,1,0:T(2,128)S(1)} %collective-permute-done.6), channel_id=1, source_target_pairs={{0,1},{1,2},{2,3},{3,4},{4,5},{5,6},{6,7},{7,8},{8,9},{9,10},{10,1... | collective-permute-start | bytes 1544 | tf_op jit(solution)/shard_map/ppermute | solution.py:17
  201.8 2.7 collective-permute-start.14
Sparse Core Ops, SparseCore 0:
  12.8 93.4 all-reduce.2
  201.9 35.7 all-gather.3
